TPU v7x, 512 devices: a whole 4x4x16 slice. The times are simulated.
512 devices in a mesh: space: 32 (over z, core), tm: 16 (over y, x).
Axes of the slice: x: 4, y: 4, z: 16, core: 2. Of those that a mesh axis runs over, the one named last changes fastest.
Arguments:
- snapshots: bfloat16 [65536, 16384], P('space', 'tm'), may hold values from -6 to 6
- basis: bfloat16 [65536, 256], P(('space', 'tm')), may hold values from -0.0234375 to 0.0234375
- lengths: int32 [16, 64], P('tm'), may hold values from 1 to 61, as said below
- owners: int32 [16, 64], P('tm'), may hold values from 0 to 31, as said below
Outputs:
- gram_out: bfloat16 [16, 32, 392, 392], P('tm', 'space')
- target_out: bfloat16 [16, 32, 392, 256], P('tm', 'space')
Inputs may be any that keep to these rules, and one draw needn't show every extreme that they name: Each row of lengths sums to 1024. The trajectories that one owner holds in one row have 62 snapshots together at most, and in every row some owner holds exactly 62. `owners`: in every row each space index owns exactly two trajectories.
All inputs are finite; a program needn't handle non-finite values.
Results may differ from a plain program's by a relative error of at most 0.0057.
Values may be sent and summed in bfloat16 or wider, within the bound.
No kernel may reach another device: no remote copies, remote signals or barrier semaphores. Data moves between devices by JAX's collectives and lax.ppermute only.
A program may use at most 64 MiB of HBM per device.

v0:
```python
import jax
import jax.numpy as jnp
import numpy as np
from jax import lax
from jax.sharding import PartitionSpec as P

QM = 16


def slot_plan(length_row, owner_row, owner_count, capacity, snap_count):
    traj_end = jnp.cumsum(length_row)
    starts = traj_end - length_row
    snap_index = jnp.arange(snap_count, dtype=jnp.int32)
    member = (
        (snap_index[:, None] >= starts[None, :]) & (snap_index[:, None] < traj_end[None, :])
    ).astype(jnp.int32)
    snap_start = jnp.sum(member * starts[None, :], axis=1)
    snap_end = jnp.sum(member * traj_end[None, :], axis=1)
    snap_owner = jnp.sum(member * owner_row[None, :], axis=1)
    traj_index = jnp.arange(length_row.shape[0], dtype=jnp.int32)
    same_owner = owner_row[:, None] == owner_row[None, :]
    earlier = traj_index[None, :] < traj_index[:, None]
    offset = jnp.sum(jnp.where(same_owner & earlier, length_row[None, :], 0), axis=1)
    slot_index = jnp.sum(member * offset[None, :], axis=1) + snap_index - snap_start
    has_next = (snap_index + 1 < snap_end).astype(jnp.int32)
    destination = snap_owner * capacity + slot_index
    source_rows = jnp.full((owner_count * capacity,), -1, jnp.int32).at[destination].set(snap_index)
    live_rows = jnp.zeros((owner_count * capacity,), jnp.int32).at[destination].set(has_next)
    return (source_rows, live_rows)


def library(coords, live_slots, weight_scale):
    first_mode, second_mode = np.triu_indices(QM)
    products = coords[:, first_mode] * coords[:, second_mode]
    library_rows = jnp.concatenate([coords, products], axis=1).astype(jnp.bfloat16)
    successor = jnp.concatenate(
        [coords[1:], jnp.zeros((1, coords.shape[1]), jnp.float32)], axis=0
    ).astype(jnp.bfloat16)
    weighted = library_rows * live_slots[:, None].astype(jnp.bfloat16)
    dims = (((0,), (0,)), ((), ()))
    gram_matrix = (
        lax.dot_general(weighted, library_rows, dims, preferred_element_type=jnp.float32)
        * weight_scale
    )
    targets = (
        lax.dot_general(weighted, successor, dims, preferred_element_type=jnp.float32)
        * weight_scale
    )
    return (gram_matrix.astype(jnp.bfloat16), targets.astype(jnp.bfloat16))


def on_device(snapshots, basis, lengths, owners):
    dims = (((0,), (0,)), ((), ()))
    snap_count = snapshots.shape[1]
    gathered = lax.all_gather(basis, "tm", axis=0, tiled=True)
    partial_value = lax.dot_general(snapshots, gathered, dims, preferred_element_type=jnp.float32)
    owner_count = lax.axis_size("space")
    capacity = 2 * snap_count // owner_count - 2
    source_rows, live_rows = slot_plan(lengths[0], owners[0], owner_count, capacity, snap_count)
    own_index = lax.axis_index("space")
    mine = lax.dynamic_slice_in_dim(source_rows, own_index * capacity, capacity)
    summed = lax.psum(partial_value, "space")
    packed = jnp.take(summed, jnp.maximum(mine, 0), axis=0) * (mine >= 0)[:, None].astype(
        jnp.float32
    )
    live_slots = lax.dynamic_slice_in_dim(live_rows, own_index * capacity, capacity)
    gram_matrix, targets = library(packed, live_slots, owner_count / snap_count)
    return (gram_matrix[None, None], targets[None, None])


def solution(mesh):
    placed = (P("space", "tm"), P(("space", "tm"), None), P("tm", None), P("tm", None))
    return jax.shard_map(
        on_device,
        mesh=mesh,
        in_specs=placed,
        out_specs=(P("tm", "space", None, None), P("tm", "space", None, None)),
        check_vma=False,
    )
```

profile of v0, /device:TPU:1, one launch (start us, length us, event | category | flops | bytes accessed | tf_op | source)
XLA Modules:
  0.0 301.7 jit_solution(7914927873324652971)
XLA Ops:
  7.2 0.0 all-gather.2.cloned.1.call-start
  7.2 0.7 all-gather.2.cloned.1.call-update
  7.9 0.0 all-reduce.3.cloned.1.call-start
  7.9 0.7 copy.20
  8.7 0.1 reduce-window.4
  8.8 0.1 reduce
  8.9 0.9 select_reduce_fusion.4
  9.8 0.7 fusion.17
  10.5 0.8 select_reduce_fusion
  11.4 4.3 %scatter_custom_fusion.1 = s32[1984]{0:T(1024)S(1)} fusion(s32[1024]{0:T(1024)S(1)} %bitcast.28, s32[1024]{0:T(1024)S(1)} %fusion.16, s32[]{:T(128)} %constant.22.clone.1), kind=kCustom, calls=%fused_computation.35 | custom fusion | bytes 7940 | tf_op jit(solution)/shard_map/scatter | solution.py:28
  15.7 4.3 %scatter_custom_fusion = s32[1984]{0:T(1024)S(1)} fusion(s32[1024]{0:T(1024)S(1)} %bitcast.29, s32[1024]{0:T(1024)S(1)} %iota.19, s32[]{:T(128)} %constant.21.clone.1), kind=kCustom, calls=%fused_computation.37 | custom fusion | bytes 7940 | tf_op jit(solution)/shard_map/scatter | solution.py:27
  20.0 0.0 copy-start.1
  20.1 0.0 copy-start
  20.1 52.9 %all-gather.2.cloned.1.call-done = bf16[2048,256]{1,0:T(8,128)(2,1)} async-done(((bf16[128,256]{1,0:T(8,128)(2,1)}), bf16[2048,256]{1,0:T(8,128)(2,1)}) %all-gather.2.cloned.1.call-update) | async-done | bytes 1048592 | tf_op jit(solution)/shard_map/all_gather | solution.py:55
  72.9 4.8 %fusion.22 = f32[1024,256]{1,0:T(8,128)} fusion(bf16[2048,1024]{1,0:T(8,128)(2,1)} %param.8, bf16[2048,256]{1,0:T(8,128)(2,1)} %all-gather.2.cloned.1.call-done), kind=kOutput, calls=%fused_computation.51 | convolution fusion | flops 1073741824 | bytes 6291456 | tf_op jit(solution)/shard_map/dot_general | solution.py:56
  77.7 0.0 all-reduce.3.cloned.1.call-update
  77.7 0.1 dynamic-slice_convert_fusion
  77.8 0.1 broadcast_compare_fusion
  77.9 0.0 copy-done.1
  77.9 0.0 copy-done
  77.9 211.2 %all-reduce.3.cloned.1.call-done = f32[1024,256]{1,0:T(8,128)} async-done(((f32[1024,256]{1,0:T(8,128)}), f32[1024,256]{1,0:T(8,128)}) %all-reduce.3.cloned.1.call-update) | async-done | bytes 1048592 | tf_op jit(solution)/shard_map/psum | solution.py:62
  289.2 1.9 gather_fusion
  291.0 0.1 fusion.21
  291.1 0.1 copy.21
  291.2 0.7 gather_fusion.2
  291.9 0.7 gather_fusion.1
  292.6 0.1 copy.23
  292.7 0.1 copy.24
  292.8 1.1 fusion.1
  293.9 1.0 fusion.3
  (9 shorter events, 0.1 us)
Async XLA Ops:
  7.2 65.8 %all-gather.2.cloned.1.call-start = ((), (), s32[]{:S(2)}) async-start(), calls=%async_computation | async-start | bytes 1114112 | tf_op jit(solution)/shard_map/all_gather | solution.py:55
  7.9 281.3 %all-reduce.3.cloned.1.call-start = ((), (), s32[]{:S(2)}) async-start(), calls=%async_computation.1 | async-start | bytes 2097152 | tf_op jit(solution)/shard_map/psum | solution.py:62
  20.0 57.8 %copy-start.1 = (s32[136]{0:T(256)S(1)}, s32[136]{0:T(256)}, u32[]{:S(2)}) copy-start(s32[136]{0:T(256)} %constant.68) | copy-start | bytes 1636
  20.1 57.8 %copy-start = (s32[136]{0:T(256)S(1)}, s32[136]{0:T(256)}, u32[]{:S(2)}) copy-start(s32[136]{0:T(256)} %constant.69) | copy-start | bytes 1636
Sparse Core Ops, SparseCore 0:
  11.0 61.8 all-gather.1
  77.8 211.2 all-reduce.2
where the time goes:
time: 302 us
  waiting for transfers between devices  265 us (88%)
  between operations  14.2 us (5%)
  local copies, waits for them, and re-layouts  12.9 us (4%)
  matrix products  6.86 us (2%)
    psum x1, waiting for transfers between devices, on_device(): summed = lax.psum(partial_value, 'space')  211 us
    all_gather x1, waiting for transfers between devices, on_device(): gathered = lax.all_gather(basis, 'tm', axis=0, tiled=True)  52.9 us
  transfers between devices with their start and end apart: 2, of which 2 were waited for; matrix products, arithmetic and copies ran while one was open for 4% of the time, Pallas kernels for 0%

commit v1 on v0

--- a/solution.py
+++ b/solution.py
@@ -52,7 +52,24 @@
 def on_device(snapshots, basis, lengths, owners):
     dims = (((0,), (0,)), ((), ()))
     snap_count = snapshots.shape[1]
-    gathered = lax.all_gather(basis, "tm", axis=0, tiled=True)
+    length, position, rows = (lax.axis_size("tm"), lax.axis_index("tm"), basis.shape[0])
+    upward = [(i, (i + 1) % length) for i in range(length)]
+    backward = [(i, (i - 1) % length) for i in range(length)]
+    out = jnp.zeros((*basis.shape[:0], length * rows, *basis.shape[0 + 1 :]), basis.dtype)
+    out = lax.dynamic_update_slice_in_dim(out, basis, position * rows, axis=0)
+    from_left = from_right = basis
+    halfway = length // 2
+    for step in range(1, halfway + 1):
+        from_left = lax.ppermute(from_left, "tm", upward)
+        out = lax.dynamic_update_slice_in_dim(
+            out, from_left, (position - step) % length * rows, axis=0
+        )
+        if step < length - halfway:
+            from_right = lax.ppermute(from_right, "tm", backward)
+            out = lax.dynamic_update_slice_in_dim(
+                out, from_right, (position + step) % length * rows, axis=0
+            )
+    gathered = out
     partial_value = lax.dot_general(snapshots, gathered, dims, preferred_element_type=jnp.float32)
     owner_count = lax.axis_size("space")
     capacity = 2 * snap_count // owner_count - 2

time: 302 us -> 325 us (1.076)
  starting transfers between devices: 0.08 us -> 63.4 us
  waiting for transfers between devices: 265 us -> 222 us
    ppermute x0 -> x15, starting transfers between devices: none -> 63.4 us  [the longest x7 46 us: on_device(): from_right = lax.ppermute(from_right, 'tm', backward)]
    all_gather x1 -> x0, waiting for transfers between devices: 52.9 us -> none  [on_device(): gathered = lax.all_gather(basis, 'tm', axis=0, tiled=True)]
    ppermute x0 -> x15, waiting for transfers between devices: none -> 6.66 us  [the longest x8 6.64 us: on_device(): from_left = lax.ppermute(from_left, 'tm', upward)]
    psum x1, waiting for transfers between devices: 211 us -> 216 us  [on_device(): summed = lax.psum(partial_value, 'space')]
  transfers between devices with their start and end apart: 2 -> 16, of which waited for: 2 -> 3; matrix products, arithmetic and copies ran while one was open for 4% -> 4% of each run, Pallas kernels for 0% -> 0%
where the time goes in v1:
time: 325 us; the launch traced here: 324 us
  waiting for transfers between devices  222 us (68%)
  starting transfers between devices  63.4 us (20%)
  between operations  14.9 us (5%)
  local copies, waits for them, and re-layouts  14.3 us (4%)
  matrix products  6.61 us (2%)
    psum x1, waiting for transfers between devices, on_device(): summed = lax.psum(partial_value, 'space')  216 us
    ppermute x7, starting transfers between devices, on_device(): from_right = lax.ppermute(from_right, 'tm', backward)  46 us
    ppermute x8, starting transfers between devices, on_device(): from_left = lax.ppermute(from_left, 'tm', upward)  17.4 us
    ppermute x8, waiting for transfers between devices, on_device(): from_left = lax.ppermute(from_left, 'tm', upward)  6.64 us
  transfers between devices with their start and end apart: 16, of which 3 were waited for; matrix products, arithmetic and copies ran while one was open for 4% of the time, Pallas kernels for 0%

profile of v1, /device:TPU:1, one launch (start us, length us, event | category | flops | bytes accessed | tf_op | source)
XLA Modules:
  0.0 324.4 jit_solution(5802631841943797560)
XLA Ops:
  7.2 0.0 all-reduce.3.cloned.1.call-start
  7.2 4.0 %collective-permute-start = (bf16[128,256]{1,0:T(8,128)(2,1)}, bf16[128,256]{1,0:T(8,128)(2,1)S(1)}, u32[]{:S(2)}, u32[]{:S(2)}) collective-permute-start(bf16[128,256]{1,0:T(8,128)(2,1)} %param.9), channel_id=1, source_target_pairs={{0,1},{1,2},{2,3},{3,4},{4,5},{5,6},{6,7},{7,8},{8,9},{9,10},{10,1... | collective-permute-start | bytes 196616 | tf_op jit(solution)/shard_map/ppermute | solution.py:63
  11.2 5.6 %collective-permute-start.1 = (bf16[128,256]{1,0:T(8,128)(2,1)}, bf16[128,256]{1,0:T(8,128)(2,1)S(1)}, u32[]{:S(2)}, u32[]{:S(2)}) collective-permute-start(bf16[128,256]{1,0:T(8,128)(2,1)} %param.9), channel_id=1, source_target_pairs={{0,15},{1,0},{2,1},{3,2},{4,3},{5,4},{6,5},{7,6},{8,7},{9,8},{10,9... | collective-permute-start | bytes 196616 | tf_op jit(solution)/shard_map/ppermute | solution.py:68
  17.1 0.7 copy.22
  17.8 0.1 reduce-window.4
  17.9 0.1 reduce
  18.0 0.7 fusion.17
  18.7 0.9 select_reduce_fusion.4
  19.6 0.9 select_reduce_fusion
  20.5 4.3 %scatter_custom_fusion = s32[1984]{0:T(1024)S(1)} fusion(s32[1024]{0:T(1024)S(1)} %bitcast.28, s32[1024]{0:T(1024)S(1)} %iota.19, s32[]{:T(128)} %constant.133.clone.1), kind=kCustom, calls=%fused_computation.54 | custom fusion | bytes 7940 | tf_op jit(solution)/shard_map/scatter | solution.py:27
  24.9 4.3 %scatter_custom_fusion.1 = s32[1984]{0:T(1024)S(1)} fusion(s32[1024]{0:T(1024)S(1)} %bitcast.29, s32[1024]{0:T(1024)S(1)} %fusion.16, s32[]{:T(128)} %constant.134.clone.1), kind=kCustom, calls=%fused_computation.36 | custom fusion | bytes 7940 | tf_op jit(solution)/shard_map/scatter | solution.py:28
  29.3 0.1 broadcast_in_dim.66
  29.3 0.9 constant_dynamic-update-slice_fusion.15
  30.2 0.0 collective-permute-done
  30.2 1.9 collective-permute-start.2
  32.1 0.0 collective-permute-done.1
  32.1 6.7 %collective-permute-start.3 = (bf16[128,256]{1,0:T(8,128)(2,1)S(1)}, bf16[128,256]{1,0:T(8,128)(2,1)S(1)}, u32[]{:S(2)}, u32[]{:S(2)}) collective-permute-start(bf16[128,256]{1,0:T(8,128)(2,1)S(1)} %collective-permute-done.1), channel_id=1, source_target_pairs={{0,15},{1,0},{2,1},{3,2},{4,3},{5,4},{6,5},{7,6},{8,7},{9,8},{10,9... | collective-permute-start | bytes 196616 | tf_op jit(solution)/shard_map/ppermute | solution.py:68
  38.9 0.0 collective-permute-done.2
  38.9 1.9 collective-permute-start.4
  40.8 0.0 collective-permute-done.3
  40.8 6.7 %collective-permute-start.5 = (bf16[128,256]{1,0:T(8,128)(2,1)S(1)}, bf16[128,256]{1,0:T(8,128)(2,1)S(1)}, u32[]{:S(2)}, u32[]{:S(2)}) collective-permute-start(bf16[128,256]{1,0:T(8,128)(2,1)S(1)} %collective-permute-done.3), channel_id=1, source_target_pairs={{0,15},{1,0},{2,1},{3,2},{4,3},{5,4},{6,5},{7,6},{8,7},{9,8},{10,9... | collective-permute-start | bytes 196616 | tf_op jit(solution)/shard_map/ppermute | solution.py:68
  47.5 0.0 collective-permute-done.4
  47.6 1.9 collective-permute-start.6
  49.5 0.0 collective-permute-done.5
  49.5 6.7 %collective-permute-start.7 = (bf16[128,256]{1,0:T(8,128)(2,1)S(1)}, bf16[128,256]{1,0:T(8,128)(2,1)S(1)}, u32[]{:S(2)}, u32[]{:S(2)}) collective-permute-start(bf16[128,256]{1,0:T(8,128)(2,1)S(1)} %collective-permute-done.5), channel_id=1, source_target_pairs={{0,15},{1,0},{2,1},{3,2},{4,3},{5,4},{6,5},{7,6},{8,7},{9,8},{10,9... | collective-permute-start | bytes 196616 | tf_op jit(solution)/shard_map/ppermute | solution.py:68
  56.2 0.0 collective-permute-done.6
  56.2 1.9 collective-permute-start.8
  58.2 0.0 collective-permute-done.7
  58.2 6.7 %collective-permute-start.9 = (bf16[128,256]{1,0:T(8,128)(2,1)S(1)}, bf16[128,256]{1,0:T(8,128)(2,1)S(1)}, u32[]{:S(2)}, u32[]{:S(2)}) collective-permute-start(bf16[128,256]{1,0:T(8,128)(2,1)S(1)} %collective-permute-done.7), channel_id=1, source_target_pairs={{0,15},{1,0},{2,1},{3,2},{4,3},{5,4},{6,5},{7,6},{8,7},{9,8},{10,9... | collective-permute-start | bytes 196616 | tf_op jit(solution)/shard_map/ppermute | solution.py:68
  64.9 0.3 collective-permute-done.8
  65.2 1.9 collective-permute-start.10
  67.1 0.0 collective-permute-done.9
  67.1 7.0 %collective-permute-start.11 = (bf16[128,256]{1,0:T(8,128)(2,1)S(1)}, bf16[128,256]{1,0:T(8,128)(2,1)S(1)}, u32[]{:S(2)}, u32[]{:S(2)}) collective-permute-start(bf16[128,256]{1,0:T(8,128)(2,1)S(1)} %collective-permute-done.9), channel_id=1, source_target_pairs={{0,15},{1,0},{2,1},{3,2},{4,3},{5,4},{6,5},{7,6},{8,7},{9,8},{10,9... | collective-permute-start | bytes 196616 | tf_op jit(solution)/shard_map/ppermute | solution.py:68
  74.1 0.0 collective-permute-done.10
  74.1 1.9 collective-permute-start.12
  76.1 0.0 collective-permute-done.11
  76.1 6.7 %collective-permute-start.13 = (bf16[128,256]{1,0:T(8,128)(2,1)S(1)}, bf16[128,256]{1,0:T(8,128)(2,1)S(1)}, u32[]{:S(2)}, u32[]{:S(2)}) collective-permute-start(bf16[128,256]{1,0:T(8,128)(2,1)S(1)} %collective-permute-done.11), channel_id=1, source_target_pairs={{0,15},{1,0},{2,1},{3,2},{4,3},{5,4},{6,5},{7,6},{8,7},{9,8},{10,9... | collective-permute-start | bytes 196616 | tf_op jit(solution)/shard_map/ppermute | solution.py:68
  82.8 0.0 collective-permute-done.12
  82.8 1.9 collective-permute-start.14
  84.8 0.0 collective-permute-done.13
  84.8 6.4 %collective-permute-done.14 = bf16[128,256]{1,0:T(8,128)(2,1)S(1)} collective-permute-done((bf16[128,256]{1,0:T(8,128)(2,1)S(1)}, bf16[128,256]{1,0:T(8,128)(2,1)S(1)}, u32[]{:S(2)}, u32[]{:S(2)}) %collective-permute-start.14) | collective-permute-done | bytes 65568 | tf_op jit(solution)/shard_map/ppermute | solution.py:63
  91.2 0.0 copy-start.1
  91.2 0.0 copy-start
  91.2 4.5 %convolution_bitcast_fusion = f32[1024,256]{0,1:T(8,128)} fusion(bf16[2048,256]{1,0:T(8,128)(2,1)S(1)} %constant_dynamic-update-slice_fusion, bf16[2048,1024]{1,0:T(8,128)(2,1)} %param.8), kind=kOutput, calls=%fused_computation.5 | convolution fusion | flops 1073741824 | bytes 6291456 | tf_op jit(solution)/shard_map/dot_general | solution.py:73
  95.7 0.0 all-reduce.3.cloned.1.call-update
  95.7 0.1 dynamic-slice_convert_fusion
  95.8 0.1 broadcast_compare_fusion
  95.9 0.0 copy-done.1
  95.9 0.0 copy-done
  95.9 215.6 %all-reduce.3.cloned.1.call-done = f32[1024,256]{0,1:T(8,128)} async-done(((f32[1024,256]{0,1:T(8,128)}), f32[1024,256]{0,1:T(8,128)}) %all-reduce.3.cloned.1.call-update) | async-done | bytes 1048592 | tf_op jit(solution)/shard_map/psum | solution.py:79
  311.5 1.6 copy.23
  313.1 0.7 gather_fusion
  313.7 0.1 fusion.21
  313.8 0.1 copy.24
  313.9 0.7 gather_fusion.1
  314.6 0.1 copy.26
  314.7 0.7 gather_fusion.2
  315.3 0.1 copy.27
  315.5 1.1 fusion.1
  316.6 1.0 fusion.3
  (24 shorter events, 0.2 us)
Async XLA Ops:
  7.2 304.3 %all-reduce.3.cloned.1.call-start = ((), (), s32[]{:S(2)}) async-start(), calls=%async_computation | async-start | bytes 2097152 | tf_op jit(solution)/shard_map/psum | solution.py:79
  7.2 23.0 %collective-permute-start = (bf16[128,256]{1,0:T(8,128)(2,1)}, bf16[128,256]{1,0:T(8,128)(2,1)S(1)}, u32[]{:S(2)}, u32[]{:S(2)}) collective-permute-start(bf16[128,256]{1,0:T(8,128)(2,1)} %param.9), channel_id=1, source_target_pairs={{0,1},{1,2},{2,3},{3,4},{4,5},{5,6},{6,7},{7,8},{8,9},{9,10},{10,1... | collective-permute-start | bytes 196616 | tf_op jit(solution)/shard_map/ppermute | solution.py:63
  11.2 21.0 %collective-permute-start.1 = (bf16[128,256]{1,0:T(8,128)(2,1)}, bf16[128,256]{1,0:T(8,128)(2,1)S(1)}, u32[]{:S(2)}, u32[]{:S(2)}) collective-permute-start(bf16[128,256]{1,0:T(8,128)(2,1)} %param.9), channel_id=1, source_target_pairs={{0,15},{1,0},{2,1},{3,2},{4,3},{5,4},{6,5},{7,6},{8,7},{9,8},{10,9... | collective-permute-start | bytes 196616 | tf_op jit(solution)/shard_map/ppermute | solution.py:68
  30.2 8.7 %collective-permute-start.2 = (bf16[128,256]{1,0:T(8,128)(2,1)S(1)}, bf16[128,256]{1,0:T(8,128)(2,1)S(1)}, u32[]{:S(2)}, u32[]{:S(2)}) collective-permute-start(bf16[128,256]{1,0:T(8,128)(2,1)S(1)} %collective-permute-done), channel_id=1, source_target_pairs={{0,1},{1,2},{2,3},{3,4},{4,5},{5,6},{6,7},{7,8},{8,9},{9,10},{10,1... | collective-permute-start | bytes 196616 | tf_op jit(solution)/shard_map/ppermute | solution.py:63
  32.1 8.7 %collective-permute-start.3 = (bf16[128,256]{1,0:T(8,128)(2,1)S(1)}, bf16[128,256]{1,0:T(8,128)(2,1)S(1)}, u32[]{:S(2)}, u32[]{:S(2)}) collective-permute-start(bf16[128,256]{1,0:T(8,128)(2,1)S(1)} %collective-permute-done.1), channel_id=1, source_target_pairs={{0,15},{1,0},{2,1},{3,2},{4,3},{5,4},{6,5},{7,6},{8,7},{9,8},{10,9... | collective-permute-start | bytes 196616 | tf_op jit(solution)/shard_map/ppermute | solution.py:68
  38.9 8.7 %collective-permute-start.4 = (bf16[128,256]{1,0:T(8,128)(2,1)S(1)}, bf16[128,256]{1,0:T(8,128)(2,1)S(1)}, u32[]{:S(2)}, u32[]{:S(2)}) collective-permute-start(bf16[128,256]{1,0:T(8,128)(2,1)S(1)} %collective-permute-done.2), channel_id=1, source_target_pairs={{0,1},{1,2},{2,3},{3,4},{4,5},{5,6},{6,7},{7,8},{8,9},{9,10},{10,1... | collective-permute-start | bytes 196616 | tf_op jit(solution)/shard_map/ppermute | solution.py:63
  40.8 8.7 %collective-permute-start.5 = (bf16[128,256]{1,0:T(8,128)(2,1)S(1)}, bf16[128,256]{1,0:T(8,128)(2,1)S(1)}, u32[]{:S(2)}, u32[]{:S(2)}) collective-permute-start(bf16[128,256]{1,0:T(8,128)(2,1)S(1)} %collective-permute-done.3), channel_id=1, source_target_pairs={{0,15},{1,0},{2,1},{3,2},{4,3},{5,4},{6,5},{7,6},{8,7},{9,8},{10,9... | collective-permute-start | bytes 196616 | tf_op jit(solution)/shard_map/ppermute | solution.py:68
  47.6 8.7 %collective-permute-start.6 = (bf16[128,256]{1,0:T(8,128)(2,1)S(1)}, bf16[128,256]{1,0:T(8,128)(2,1)S(1)}, u32[]{:S(2)}, u32[]{:S(2)}) collective-permute-start(bf16[128,256]{1,0:T(8,128)(2,1)S(1)} %collective-permute-done.4), channel_id=1, source_target_pairs={{0,1},{1,2},{2,3},{3,4},{4,5},{5,6},{6,7},{7,8},{8,9},{9,10},{10,1... | collective-permute-start | bytes 196616 | tf_op jit(solution)/shard_map/ppermute | solution.py:63
  49.5 8.7 %collective-permute-start.7 = (bf16[128,256]{1,0:T(8,128)(2,1)S(1)}, bf16[128,256]{1,0:T(8,128)(2,1)S(1)}, u32[]{:S(2)}, u32[]{:S(2)}) collective-permute-start(bf16[128,256]{1,0:T(8,128)(2,1)S(1)} %collective-permute-done.5), channel_id=1, source_target_pairs={{0,15},{1,0},{2,1},{3,2},{4,3},{5,4},{6,5},{7,6},{8,7},{9,8},{10,9... | collective-permute-start | bytes 196616 | tf_op jit(solution)/shard_map/ppermute | solution.py:68
  56.2 8.9 %collective-permute-start.8 = (bf16[128,256]{1,0:T(8,128)(2,1)S(1)}, bf16[128,256]{1,0:T(8,128)(2,1)S(1)}, u32[]{:S(2)}, u32[]{:S(2)}) collective-permute-start(bf16[128,256]{1,0:T(8,128)(2,1)S(1)} %collective-permute-done.6), channel_id=1, source_target_pairs={{0,1},{1,2},{2,3},{3,4},{4,5},{5,6},{6,7},{7,8},{8,9},{9,10},{10,1... | collective-permute-start | bytes 196616 | tf_op jit(solution)/shard_map/ppermute | solution.py:63
  58.2 8.9 %collective-permute-start.9 = (bf16[128,256]{1,0:T(8,128)(2,1)S(1)}, bf16[128,256]{1,0:T(8,128)(2,1)S(1)}, u32[]{:S(2)}, u32[]{:S(2)}) collective-permute-start(bf16[128,256]{1,0:T(8,128)(2,1)S(1)} %collective-permute-done.7), channel_id=1, source_target_pairs={{0,15},{1,0},{2,1},{3,2},{4,3},{5,4},{6,5},{7,6},{8,7},{9,8},{10,9... | collective-permute-start | bytes 196616 | tf_op jit(solution)/shard_map/ppermute | solution.py:68
  65.2 8.9 %collective-permute-start.10 = (bf16[128,256]{1,0:T(8,128)(2,1)S(1)}, bf16[128,256]{1,0:T(8,128)(2,1)S(1)}, u32[]{:S(2)}, u32[]{:S(2)}) collective-permute-start(bf16[128,256]{1,0:T(8,128)(2,1)S(1)} %collective-permute-done.8), channel_id=1, source_target_pairs={{0,1},{1,2},{2,3},{3,4},{4,5},{5,6},{6,7},{7,8},{8,9},{9,10},{10,1... | collective-permute-start | bytes 196616 | tf_op jit(solution)/shard_map/ppermute | solution.py:63
  67.1 9.0 %collective-permute-start.11 = (bf16[128,256]{1,0:T(8,128)(2,1)S(1)}, bf16[128,256]{1,0:T(8,128)(2,1)S(1)}, u32[]{:S(2)}, u32[]{:S(2)}) collective-permute-start(bf16[128,256]{1,0:T(8,128)(2,1)S(1)} %collective-permute-done.9), channel_id=1, source_target_pairs={{0,15},{1,0},{2,1},{3,2},{4,3},{5,4},{6,5},{7,6},{8,7},{9,8},{10,9... | collective-permute-start | bytes 196616 | tf_op jit(solution)/shard_map/ppermute | solution.py:68
  74.1 8.7 %collective-permute-start.12 = (bf16[128,256]{1,0:T(8,128)(2,1)S(1)}, bf16[128,256]{1,0:T(8,128)(2,1)S(1)}, u32[]{:S(2)}, u32[]{:S(2)}) collective-permute-start(bf16[128,256]{1,0:T(8,128)(2,1)S(1)} %collective-permute-done.10), channel_id=1, source_target_pairs={{0,1},{1,2},{2,3},{3,4},{4,5},{5,6},{6,7},{7,8},{8,9},{9,10},{10,1... | collective-permute-start | bytes 196616 | tf_op jit(solution)/shard_map/ppermute | solution.py:63
  76.1 8.7 %collective-permute-start.13 = (bf16[128,256]{1,0:T(8,128)(2,1)S(1)}, bf16[128,256]{1,0:T(8,128)(2,1)S(1)}, u32[]{:S(2)}, u32[]{:S(2)}) collective-permute-start(bf16[128,256]{1,0:T(8,128)(2,1)S(1)} %collective-permute-done.11), channel_id=1, source_target_pairs={{0,15},{1,0},{2,1},{3,2},{4,3},{5,4},{6,5},{7,6},{8,7},{9,8},{10,9... | collective-permute-start | bytes 196616 | tf_op jit(solution)/shard_map/ppermute | solution.py:68
  82.8 8.3 %collective-permute-start.14 = (bf16[128,256]{1,0:T(8,128)(2,1)S(1)}, bf16[128,256]{1,0:T(8,128)(2,1)S(1)}, u32[]{:S(2)}, u32[]{:S(2)}) collective-permute-start(bf16[128,256]{1,0:T(8,128)(2,1)S(1)} %collective-permute-done.12), channel_id=1, source_target_pairs={{0,1},{1,2},{2,3},{3,4},{4,5},{5,6},{6,7},{7,8},{8,9},{9,10},{10,1... | collective-permute-start | bytes 196616 | tf_op jit(solution)/shard_map/ppermute | solution.py:63
  91.2 4.7 %copy-start.1 = (s32[136]{0:T(256)S(1)}, s32[136]{0:T(256)}, u32[]{:S(2)}) copy-start(s32[136]{0:T(256)} %constant.173) | copy-start | bytes 1636
  91.2 4.7 %copy-start = (s32[136]{0:T(256)S(1)}, s32[136]{0:T(256)}, u32[]{:S(2)}) copy-start(s32[136]{0:T(256)} %constant.174) | copy-start | bytes 1636
Sparse Core Ops, SparseCore 0:
  95.8 215.6 all-reduce.2
